TPU v7x, 256 devices: a whole 4x4x8 slice. The times are simulated.
256 devices in a mesh: row: 8 (over x, y_hi), grp: 32 (over z, y_lo, core).
Axes of the slice: x: 4, y: 4 (y_hi: 2, y_lo: 2; y = y_hi * 2 + y_lo), z: 8, core: 2. Of those that a mesh axis runs over, the one named last changes fastest.
Arguments:
- segments: bfloat16 [32, 128, 128, 512], P('grp', 'row'), may hold values from -40 to 40
- conv_weight: bfloat16 [3, 512, 512], replicated, may hold values from -0.15625 to 0.15625
- gain: float32 [512], replicated, may hold values from 0.1 to 1.9
- head: bfloat16 [512, 128], replicated, may hold values from -0.25 to 0.25
- group: int32 [32, 128], P('grp', 'row'), may hold values from 0 to 7
- positive: int32 [32, 128], P('grp', 'row'), may hold values from 0 to 127, as said below
Outputs:
- grad_conv: float32 [3, 512, 512], replicated
- grad_gain: float32 [512], replicated
- projector_derivative: float32 [512, 128], replicated
Inputs may be any that keep to these rules, and one draw needn't show every extreme that they name: positive[c, i] is another segment of the same index c with the same group, and positive[c, positive[c, i]] == i.
All inputs are finite; a program needn't handle non-finite values.
Results may differ from a plain program's by a relative error of at most 0.003.
The roundings to bfloat16 on the way count: a program that leaves them out, or rounds other values in their place, can miss the bound.
Values sent between devices are 32-bit elements; how exact they have to be, the bound alone decides.
No kernel may reach another device: no remote copies, remote signals or barrier semaphores. Data moves between devices by JAX's collectives and lax.ppermute only.
A program may use at most 64 MiB of HBM per device.

v0:
```python
from functools import partial
import jax
import jax.numpy as jnp
from jax import lax
from jax.sharding import PartitionSpec as P

DILATION_GAP = 2
logit_divisor = 0.1


def unit_rows(values):
    return values * lax.rsqrt(jnp.mean(values * values, axis=-1, keepdims=True) + 1e-05)


def scale_embed(projected):
    return unit_rows(projected) * projected.shape[-1] ** (-0.5)


def filter_tap_window(normalized_rows, filter_tap_index, spacing):
    sequence_length = normalized_rows.shape[1]
    padded = jnp.pad(normalized_rows, ((0, 0), (spacing, spacing), (0, 0)))
    return padded[:, filter_tap_index * spacing : filter_tap_index * spacing + sequence_length]


def reverse_tap_gather(term, filter_tap_index, spacing):
    sequence_length = term.shape[1]
    padded = jnp.pad(term, ((0, 0), (spacing, spacing), (0, 0)))
    begin = (2 - filter_tap_index) * spacing
    return padded[:, begin : begin + sequence_length]


def encode(patient_piece_records, conv_weight, gain, head):
    inputs = patient_piece_records.astype(jnp.float32)
    unit = unit_rows(inputs)
    normalized_rows = (unit * gain).astype(jnp.bfloat16)
    segment_count, sequence_length, channel_count = normalized_rows.shape
    conv = jnp.zeros((segment_count * sequence_length, channel_count), jnp.float32)
    for filter_tap_index in range(conv_weight.shape[0]):
        shifted_input = filter_tap_window(normalized_rows, filter_tap_index, DILATION_GAP).reshape(
            segment_count * sequence_length, channel_count
        )
        conv = conv + jnp.dot(
            shifted_input, conv_weight[filter_tap_index], preferred_element_type=jnp.float32
        )
    conv = conv.reshape(segment_count, sequence_length, channel_count)
    hidden = inputs + jax.nn.gelu(conv, approximate=True)
    pooled = jnp.mean(hidden, axis=1).astype(jnp.bfloat16)
    projected = jnp.dot(pooled, head, preferred_element_type=jnp.float32)
    return (unit, normalized_rows, conv, pooled, projected)


def backward(embed_grad, unit, normalized_rows, conv, pooled, projected, conv_weight, head):
    projected_grad = jax.vjp(scale_embed, projected)[1](embed_grad)[0]
    projector_derivative = jnp.dot(
        pooled.astype(jnp.float32).T, projected_grad, precision=lax.Precision.HIGHEST
    )
    pooled_grad = jnp.dot(
        projected_grad, head.astype(jnp.float32).T, precision=lax.Precision.HIGHEST
    )
    segment_count, sequence_length, channel_count = conv.shape
    hidden_grad = jnp.broadcast_to(pooled_grad[:, None, :] / sequence_length, conv.shape)
    conv_grad = jax.vjp(partial(jax.nn.gelu, approximate=True), conv)[1](hidden_grad)[0].astype(
        jnp.bfloat16
    )
    flat_grad = conv_grad.reshape(segment_count * sequence_length, channel_count)
    tap_grads = []
    normalized_gradient = jnp.zeros((segment_count, sequence_length, channel_count), jnp.float32)
    for filter_tap_index in range(conv_weight.shape[0]):
        shifted_input = filter_tap_window(normalized_rows, filter_tap_index, DILATION_GAP).reshape(
            segment_count * sequence_length, channel_count
        )
        tap_grads.append(
            lax.dot_general(
                shifted_input,
                flat_grad,
                (((0,), (0,)), ((), ())),
                preferred_element_type=jnp.float32,
            )
        )
        backward_term = lax.dot_general(
            flat_grad,
            conv_weight[filter_tap_index],
            (((1,), (1,)), ((), ())),
            preferred_element_type=jnp.float32,
        )
        normalized_gradient = normalized_gradient + reverse_tap_gather(
            backward_term.reshape(segment_count, sequence_length, channel_count),
            filter_tap_index,
            DILATION_GAP,
        )
    grad_conv = jnp.stack(tap_grads)
    grad_gain = jnp.sum(normalized_gradient * unit, axis=(0, 1))
    return (grad_conv, grad_gain, projector_derivative)


def body(segments, conv_weight, gain, head, group, positive):
    patient_piece_records = segments[0]
    group_ids = group[0]
    partners = positive[0]
    unit, normalized_rows, conv, pooled, projected = encode(
        patient_piece_records, conv_weight, gain, head
    )
    encounter_latent_vector = scale_embed(projected)
    gathered_embedding, all_groups = (
        lax.all_gather(encounter_latent_vector, "row", axis=0, tiled=True),
        lax.all_gather(group_ids, "row", axis=0, tiled=True),
    )
    local_count = encounter_latent_vector.shape[0]
    matrix_height_number = gathered_embedding.shape[0]
    global_multiplier = (matrix_height_number * lax.axis_size("grp")) ** (-0.5) / logit_divisor
    own_rows = lax.axis_index("row") * local_count + jnp.arange(local_count, dtype=jnp.int32)
    columns = jnp.arange(matrix_height_number, dtype=jnp.int32)
    cosine_affinity_matrix = (
        jnp.dot(encounter_latent_vector, gathered_embedding.T, precision=lax.Precision.HIGHEST)
        / logit_divisor
    )
    same_group = (group_ids[:, None] == all_groups[None, :]) & (
        own_rows[:, None] != columns[None, :]
    )
    log_total = jnp.log(
        jnp.sum(jnp.where(same_group, jnp.exp(cosine_affinity_matrix), 0.0), axis=1)
    )
    softmax = jnp.where(same_group, jnp.exp(cosine_affinity_matrix - log_total[:, None]), 0.0)
    row_term = jnp.dot(softmax, gathered_embedding, precision=lax.Precision.HIGHEST)
    partner_pick = (partners[:, None] == columns[None, :]).astype(jnp.float32)
    partner_embed = jnp.dot(partner_pick, gathered_embedding, precision=lax.Precision.HIGHEST)
    column_term = lax.psum_scatter(
        lax.dot_general(
            softmax,
            encounter_latent_vector,
            (((0,), (0,)), ((), ())),
            precision=lax.Precision.HIGHEST,
            preferred_element_type=jnp.float32,
        ),
        "row",
        scatter_dimension=0,
        tiled=True,
    )
    embed_grad = global_multiplier * (row_term + column_term - 2.0 * partner_embed)
    grads = backward(embed_grad, unit, normalized_rows, conv, pooled, projected, conv_weight, head)
    grads = lax.psum((grads[0], grads[1], grads[2]), ("row", "grp"))
    return (grads[0], grads[1], grads[2])


def solution(mesh):
    placed = (P("grp", "row", None, None), P(), P(), P(), P("grp", "row"), P("grp", "row"))
    return jax.shard_map(
        body, mesh=mesh, in_specs=placed, out_specs=(P(), P(), P()), check_vma=False
    )
```

profile of v0, /device:TPU:2, one launch (start us, length us, event | category | flops | bytes accessed | tf_op | source)
XLA Modules:
  0.0 477.1 jit_solution(5161826225677553854)
XLA Ops:
  7.2 0.0 copy-start
  7.2 0.0 reduce-scatter.2.cloned.1.call-start
  7.2 3.0 copy.23
  10.3 0.4 fusion.7
  10.7 0.7 fusion.5
  11.4 2.1 fusion.10
  13.5 3.2 pad_slice_fusion.2
  16.7 3.9 copy.24
  20.6 3.9 copy.25
  24.6 5.0 %fusion.45 = f32[2048,512]{1,0:T(8,128)} fusion(bf16[2048,512]{1,0:T(8,128)(2,1)} %bitcast.96, bf16[3,512,512]{2,1,0:T(8,128)(2,1)} %param.7), kind=kOutput, calls=%fused_computation.63 | convolution fusion | flops 1073741824 | bytes 6815744 | tf_op jit(solution)/shard_map/dot_general | solution.py:42
  29.6 4.3 fusion.43
  33.9 3.9 copy.26
  37.8 7.4 %add_add_fusion = f32[2048,512]{1,0:T(8,128)} fusion(f32[2048,512]{1,0:T(8,128)} %fusion.45, f32[2048,512]{1,0:T(8,128)} %fusion.43, bf16[2048,512]{1,0:T(8,128)(2,1)} %bitcast.98, bf16[3,512,512]{2,1,0:T(8,128)(2,1)} %param.7), kind=kOutput, calls=%fused_computation.44 | convolution fusion | flops 1075838976 | bytes 15204352 | tf_op jit(solution)/shard_map/dot_general | solution.py:42
  45.2 5.3 %copy.30 = f32[16,128,512]{1,2,0:T(8,128)} copy(f32[16,128,512]{2,1,0:T(8,128)} %bitcast.91) | data formatting | bytes 8388608 | tf_op jit(solution)/shard_map/reshape | solution.py:45
  50.5 3.4 fusion.8
  54.0 0.2 multiply_reduce_fusion.1
  54.2 0.0 copy-done.13
  54.2 0.6 dynamic-slice
  55.5 0.1 bitcast_dynamic-update-slice_fusion
  55.6 11.9 %all-reduce.3 = s32[128]{0:T(128)S(1)} all-reduce(s32[128]{0:T(128)S(1)} %bitcast_dynamic-update-slice_fusion), channel_id=2, replica_groups=mesh['row'=8,'grp'=32] {'row'}, use_global_device_ids=true, to_apply=%add.3 | all-reduce | flops 128 | bytes 1024
  67.5 0.1 multiply_multiply_fusion.4
  67.6 33.3 %all_gather.7 = f32[128,128]{1,0:T(8,128)S(1)} all-gather(f32[16,128]{1,0:T(8,128)S(1)} %multiply_multiply_fusion.4), channel_id=1, replica_groups=mesh['row'=8,'grp'=32] {'row'}, dimensions={0}, use_global_device_ids=true | all-gather | bytes 73728 | tf_op jit(solution)/shard_map/all_gather | solution.py:105
  100.9 0.3 select_reduce_fusion
  101.3 1.0 fusion.56
  102.3 0.0 reduce-scatter.2.cloned.1.call-update
  102.3 0.2 all-reduce.7.cloned.1.call-start
  102.5 78.2 %reduce-scatter.2.cloned.1.call-done = f32[16,128]{1,0:T(8,128)} async-done(((f32[128,128]{1,0:T(8,128)}), f32[16,128]{1,0:T(8,128)}) %reduce-scatter.2.cloned.1.call-update) | async-done | bytes 8208 | tf_op jit(solution)/shard_map/reduce_scatter | solution.py:127
  180.7 1.1 convolution_add_fusion
  181.8 0.0 copy-done.11
  181.8 0.3 multiply_reduce_fusion
  182.1 0.3 broadcast_multiply_fusion
  182.4 6.5 %fusion.17 = bf16[16,128,512]{1,2,0:T(8,128)(2,1)S(1)} fusion(f32[16,128,512]{1,2,0:T(8,128)} %copy.30, f32[16,512]{1,0:T(8,128)S(1)} %get-tuple-element.8, f32[16,512]{1,0:T(8,128)S(1)} %get-tuple-element.7), kind=kLoop, calls=%fused_computation.27 | loop fusion | flops 19922944 | bytes 6356992 | tf_op jit(solution)/shard_map/convert_element_type | solution.py:62
  188.9 2.7 fusion.24
  191.6 1.3 convolution_bitcast_fusion
  192.9 1.3 convolution_bitcast_fusion.1
  194.2 1.0 fusion.54
  195.2 1.2 fusion.33
  196.5 2.0 pad_maximum_fusion
  198.4 0.0 all-reduce.7.cloned.1.call-update
  198.5 0.0 copy-start.8
  198.5 3.1 fusion.40
  201.6 1.3 fusion.37
  202.9 2.6 fusion.6
  205.5 75.3 %psum.22 = f32[512]{0:T(512)} all-reduce(f32[512]{0:T(512)S(1)} %fusion.6), channel_id=1, replica_groups=mesh['row'=8,'grp'=32] {'row','grp'}, use_global_device_ids=true, to_apply=%region_8.9 | all-reduce | flops 512 | bytes 4096 | tf_op jit(solution)/shard_map/psum | solution.py:141
  280.8 184.9 %all-reduce.7.cloned.1.call-done = (f32[3,512,512]{2,1,0:T(8,128)}, f32[512,128]{1,0:T(8,128)}) async-done(((f32[3,512,512]{2,1,0:T(8,128)}, f32[512,128]{1,0:T(8,128)}), (f32[3,512,512]{2,1,0:T(8,128)}, f32[512,128]{1,0:T(8,128)})) %all-reduce.7.cloned.1.call-update) | async-done | bytes 3407888 | tf_op jit(solution)/shard_map/psum | solution.py:141
  465.7 3.9 copy.50
  469.6 0.0 copy-done.9
  469.6 0.7 copy.51
  (29 shorter events, 0.1 us)
Async XLA Ops:
  7.2 46.8 %copy-start = (bf16[512,128]{1,0:T(8,128)(2,1)S(1)}, bf16[512,128]{1,0:T(8,128)(2,1)}, u32[]{:S(2)}) copy-start(bf16[512,128]{1,0:T(8,128)(2,1)} %param.9) | copy-start | bytes 393220
  7.2 3.5 copy-start.10
  7.2 173.5 %reduce-scatter.2.cloned.1.call-start = ((), (), s32[]{:S(2)}) async-start(), calls=%async_computation.1 | async-start | bytes 73728 | tf_op jit(solution)/shard_map/reduce_scatter | solution.py:127
  11.4 5.3 %copy-start.5 = (bf16[16,128,512]{1,2,0:T(8,128)(2,1)}, bf16[16,128,512]{1,2,0:T(8,128)(2,1)S(1)}, u32[]{:S(2)}) copy-start(bf16[16,128,512]{1,2,0:T(8,128)(2,1)S(1)} %fusion.5) | copy-start | bytes 6291460
  24.6 5.0 %copy-start.4 = (bf16[1,16,128,512]{3,2,1,0:T(8,128)(2,1)S(1)}, bf16[1,16,128,512]{3,2,1,0:T(8,128)(2,1)}, u32[]{:S(2)}) copy-start(bf16[1,16,128,512]{3,2,1,0:T(8,128)(2,1)} %copy.25) | copy-start | bytes 6291460
  50.5 3.7 copy-start.13
  50.5 5.0 %copy-start.12 = (s32[1,16]{1,0:T(1,128)S(1)}, s32[1,16]{1,0:T(1,128)}, u32[]{:S(2)}) copy-start(s32[1,16]{1,0:T(1,128)} %param.10) | copy-start | bytes 196
  50.5 131.3 %copy-start.11 = (s32[1,16]{1,0:T(1,128)S(1)}, s32[1,16]{1,0:T(1,128)}, u32[]{:S(2)}) copy-start(s32[1,16]{1,0:T(1,128)} %param.11) | copy-start | bytes 196
  102.3 363.4 %all-reduce.7.cloned.1.call-start = ((), (), s32[]{:S(2)}) async-start(), calls=%async_computation.2 | async-start | bytes 6815744 | tf_op jit(solution)/shard_map/psum | solution.py:141
  180.7 8.1 %copy-start.1 = (f32[2048,512]{1,0:T(8,128)S(1)}, f32[2048,512]{1,0:T(8,128)}, u32[]{:S(2)}) copy-start(f32[2048,512]{1,0:T(8,128)} %add_add_fusion) | copy-start | bytes 12582916
  188.8 2.7 copy-start.6
  191.6 3.7 copy-start.2
  192.9 2.4 copy-start.7
  198.5 3.1 copy-start.3
  198.5 3.1 copy-start.8
  465.7 3.9 copy-start.9
Sparse Core Ops, SparseCore 0:
  102.4 78.2 reduce-scatter.1
  198.6 267.0 all-reduce.6
where the time goes:
time: 478 us; the launch traced here: 477 us
  waiting for transfers between devices  263 us (55%)
  blocking collectives  121 us (25%)
  matrix products  31.8 us (7%)
  local copies, waits for them, and re-layouts  28.6 us (6%)
  other arithmetic  17.9 us (4%)
  between operations  15 us (3%)
    psum x1, waiting for transfers between devices, body(): grads = lax.psum((grads[0], grads[1], grads[2]), ('row', 'grp'))  185 us
    reduce_scatter x1, waiting for transfers between devices, body(): lax.psum_scatter(lax.dot_general(softmax, encounter_latent_vector, (((0,)...  78.2 us
    psum x1, blocking collectives, body(): grads = lax.psum((grads[0], grads[1], grads[2]), ('row', 'grp'))  75.3 us
    all_gather x1, blocking collectives, body(): lax.all_gather(encounter_latent_vector, 'row', axis=0, tiled=True)  33.3 us
    dot_general x3, matrix products, encode(): jnp.dot(shifted_input, conv_weight[filter_tap_index], preferred_element_t...  16.7 us
    unnamed x1, blocking collectives  11.9 us
    slice x3, local copies, waits for them, and re-layouts, filter_tap_window(): padded[:, filter_tap_index * spacing:filter_tap_index * spacing + sequenc...  11 us
  transfers between devices with their start and end apart: 2, of which 2 were waited for; matrix products, arithmetic and copies ran while one was open for 1% of the time, Pallas kernels for 0%

commit v1 on v0

--- a/solution.py
+++ b/solution.py
@@ -102,7 +102,12 @@
     )
     encounter_latent_vector = scale_embed(projected)
     gathered_embedding, all_groups = (
-        lax.all_gather(encounter_latent_vector, "row", axis=0, tiled=True),
+        jnp.concatenate(
+            lax.all_to_all(
+                jnp.stack([encounter_latent_vector] * lax.axis_size("row")), "row", 0, 0
+            ),
+            axis=0,
+        ),
         lax.all_gather(group_ids, "row", axis=0, tiled=True),
     )
     local_count = encounter_latent_vector.shape[0]

time: 478 us -> 452 us (0.946)
  blocking collectives: 121 us -> 87.1 us
  starting transfers between devices: 0.26 us -> 7.69 us
    all_gather x1 -> x0, blocking collectives: 33.3 us -> none  [body(): lax.all_gather(encounter_latent_vector, 'row', axis=0, tiled=True)]
    all_to_all x0 -> x1, starting transfers between devices: none -> 7.46 us  [body(): lax.all_to_all(jnp.stack([encounter_latent_vector] * lax.axis_size('row')...]
  transfers between devices with their start and end apart: 2 -> 3, of which waited for: 2 -> 2; matrix products, arithmetic and copies ran while one was open for 1% -> 2% of each run, Pallas kernels for 0% -> 0%
where the time goes in v1:
time: 452 us; the launch traced here: 451 us
  waiting for transfers between devices  262 us (58%)
  blocking collectives  87.1 us (19%)
  matrix products  31.8 us (7%)
  local copies, waits for them, and re-layouts  29.3 us (6%)
  other arithmetic  17.9 us (4%)
  between operations  14.9 us (3%)
  starting transfers between devices  7.69 us (2%)
    psum x1, waiting for transfers between devices, body(): grads = lax.psum((grads[0], grads[1], grads[2]), ('row', 'grp'))  185 us
    reduce_scatter x1, waiting for transfers between devices, body(): lax.psum_scatter(lax.dot_general(softmax, encounter_latent_vector, (((0,)...  77.4 us
    psum x1, blocking collectives, body(): grads = lax.psum((grads[0], grads[1], grads[2]), ('row', 'grp'))  75.3 us
    dot_general x3, matrix products, encode(): jnp.dot(shifted_input, conv_weight[filter_tap_index], preferred_element_t...  16.7 us
    unnamed x1, blocking collectives  11.9 us
    slice x3, local copies, waits for them, and re-layouts, filter_tap_window(): padded[:, filter_tap_index * spacing:filter_tap_index * spacing + sequenc...  11 us
    convert_element_type x2, other arithmetic, backward(): jax.vjp(partial(jax.nn.gelu, approximate=True), conv)[1](hidden_grad)[0]  9.15 us
  transfers between devices with their start and end apart: 3, of which 2 were waited for; matrix products, arithmetic and copies ran while one was open for 2% of the time, Pallas kernels for 0%

profile of v1, /device:TPU:2, one launch (start us, length us, event | category | flops | bytes accessed | tf_op | source)
XLA Modules:
  0.0 451.0 jit_solution(11084042266883020221)
XLA Ops:
  7.2 0.0 copy-start
  7.2 3.1 copy.23
  10.3 0.4 fusion.7
  10.7 0.7 fusion.5
  11.4 2.1 fusion.10
  13.5 3.2 pad_slice_fusion.2
  16.7 3.9 copy.24
  20.6 3.9 copy.25
  24.6 5.0 %fusion.45 = f32[2048,512]{1,0:T(8,128)} fusion(bf16[2048,512]{1,0:T(8,128)(2,1)} %bitcast.97, bf16[3,512,512]{2,1,0:T(8,128)(2,1)} %param.7), kind=kOutput, calls=%fused_computation.63 | convolution fusion | flops 1073741824 | bytes 6815744 | tf_op jit(solution)/shard_map/dot_general | solution.py:42
  29.6 4.3 fusion.43
  33.9 3.9 copy.26
  37.8 7.4 %add_add_fusion = f32[2048,512]{1,0:T(8,128)} fusion(f32[2048,512]{1,0:T(8,128)} %fusion.45, f32[2048,512]{1,0:T(8,128)} %fusion.43, bf16[2048,512]{1,0:T(8,128)(2,1)} %bitcast.99, bf16[3,512,512]{2,1,0:T(8,128)(2,1)} %param.7), kind=kOutput, calls=%fused_computation.44 | convolution fusion | flops 1075838976 | bytes 15204352 | tf_op jit(solution)/shard_map/dot_general | solution.py:42
  45.2 5.3 %copy.30 = f32[16,128,512]{1,2,0:T(8,128)} copy(f32[16,128,512]{2,1,0:T(8,128)} %bitcast.92) | data formatting | bytes 8388608 | tf_op jit(solution)/shard_map/reshape | solution.py:45
  50.5 3.4 fusion.8
  54.0 0.2 multiply_reduce_fusion.1
  54.2 0.1 multiply_multiply_fusion.4
  54.3 0.6 stack.10
  55.0 7.5 %all-to-all-start = ((f32[8,16,128]{2,1,0:T(8,128)}), f32[8,16,128]{2,1,0:T(8,128)S(1)}, u32[]{:S(2)}, u32[]{:S(2)}) async-start(f32[8,16,128]{2,1,0:T(8,128)} %stack.10), calls=%async_computation | async-start | bytes 131072 | tf_op jit(solution)/shard_map/all_to_all | solution.py:106
  62.4 0.0 copy-done.13
  62.4 0.6 dynamic-slice
  63.7 0.1 bitcast_dynamic-update-slice_fusion
  63.8 11.9 %all-reduce.3 = s32[128]{0:T(128)S(1)} all-reduce(s32[128]{0:T(128)S(1)} %bitcast_dynamic-update-slice_fusion), channel_id=2, replica_groups=mesh['row'=8,'grp'=32] {'row'}, use_global_device_ids=true, to_apply=%add.3 | all-reduce | flops 128 | bytes 1024
  75.7 0.0 all-to-all-done
  75.7 0.3 select_reduce_fusion
  76.0 1.0 fusion.56
  77.0 0.0 reduce-scatter.2.cloned.1.call-update
  77.1 0.2 all-reduce.7.cloned.1.call-start
  77.3 77.4 %reduce-scatter.2.cloned.1.call-done = f32[16,128]{1,0:T(8,128)} async-done(((f32[128,128]{1,0:T(8,128)}), f32[16,128]{1,0:T(8,128)}) %reduce-scatter.2.cloned.1.call-update) | async-done | bytes 8208 | tf_op jit(solution)/shard_map/reduce_scatter | solution.py:132
  154.7 1.1 convolution_add_fusion
  155.7 0.0 copy-done.11
  155.8 0.3 multiply_reduce_fusion
  156.1 0.3 broadcast_multiply_fusion
  156.4 6.5 %fusion.17 = bf16[16,128,512]{1,2,0:T(8,128)(2,1)S(1)} fusion(f32[16,128,512]{1,2,0:T(8,128)} %copy.30, f32[16,512]{1,0:T(8,128)S(1)} %get-tuple-element.8, f32[16,512]{1,0:T(8,128)S(1)} %get-tuple-element.7), kind=kLoop, calls=%fused_computation.27 | loop fusion | flops 19922944 | bytes 6356992 | tf_op jit(solution)/shard_map/convert_element_type | solution.py:62
  162.8 2.7 fusion.24
  165.6 1.3 convolution_bitcast_fusion
  166.9 1.3 convolution_bitcast_fusion.1
  168.2 1.0 fusion.54
  169.2 1.2 fusion.33
  170.5 2.0 pad_maximum_fusion
  172.4 0.0 all-reduce.7.cloned.1.call-update
  172.5 0.0 copy-start.8
  172.5 3.1 fusion.40
  175.6 1.3 fusion.37
  176.9 2.6 fusion.6
  179.5 75.3 %psum.22 = f32[512]{0:T(512)} all-reduce(f32[512]{0:T(512)S(1)} %fusion.6), channel_id=1, replica_groups=mesh['row'=8,'grp'=32] {'row','grp'}, use_global_device_ids=true, to_apply=%region_8.9 | all-reduce | flops 512 | bytes 4096 | tf_op jit(solution)/shard_map/psum | solution.py:146
  254.7 184.8 %all-reduce.7.cloned.1.call-done = (f32[3,512,512]{2,1,0:T(8,128)}, f32[512,128]{1,0:T(8,128)}) async-done(((f32[3,512,512]{2,1,0:T(8,128)}, f32[512,128]{1,0:T(8,128)}), (f32[3,512,512]{2,1,0:T(8,128)}, f32[512,128]{1,0:T(8,128)})) %all-reduce.7.cloned.1.call-update) | async-done | bytes 3407888 | tf_op jit(solution)/shard_map/psum | solution.py:146
  439.6 3.9 copy.50
  443.5 0.7 copy.51
  (31 shorter events, 0.1 us)
Async XLA Ops:
  7.2 46.8 %copy-start = (bf16[512,128]{1,0:T(8,128)(2,1)S(1)}, bf16[512,128]{1,0:T(8,128)(2,1)}, u32[]{:S(2)}) copy-start(bf16[512,128]{1,0:T(8,128)(2,1)} %param.9) | copy-start | bytes 393220
  7.2 3.5 copy-start.10
  11.4 5.3 %copy-start.5 = (bf16[16,128,512]{1,2,0:T(8,128)(2,1)}, bf16[16,128,512]{1,2,0:T(8,128)(2,1)S(1)}, u32[]{:S(2)}) copy-start(bf16[16,128,512]{1,2,0:T(8,128)(2,1)S(1)} %fusion.5) | copy-start | bytes 6291460
  24.6 5.0 %copy-start.4 = (bf16[1,16,128,512]{3,2,1,0:T(8,128)(2,1)S(1)}, bf16[1,16,128,512]{3,2,1,0:T(8,128)(2,1)}, u32[]{:S(2)}) copy-start(bf16[1,16,128,512]{3,2,1,0:T(8,128)(2,1)} %copy.25) | copy-start | bytes 6291460
  50.5 11.9 %copy-start.13 = (u32[256]{0:T(256)S(1)}, u32[256]{0:T(256)}, u32[]{:S(2)}) copy-start(u32[256]{0:T(256)} %constant.65) | copy-start | bytes 3076
  50.5 13.2 %copy-start.12 = (s32[1,16]{1,0:T(1,128)S(1)}, s32[1,16]{1,0:T(1,128)}, u32[]{:S(2)}) copy-start(s32[1,16]{1,0:T(1,128)} %param.10) | copy-start | bytes 196
  50.5 105.2 %copy-start.11 = (s32[1,16]{1,0:T(1,128)S(1)}, s32[1,16]{1,0:T(1,128)}, u32[]{:S(2)}) copy-start(s32[1,16]{1,0:T(1,128)} %param.11) | copy-start | bytes 196
  55.0 20.7 %all-to-all-start = ((f32[8,16,128]{2,1,0:T(8,128)}), f32[8,16,128]{2,1,0:T(8,128)S(1)}, u32[]{:S(2)}, u32[]{:S(2)}) async-start(f32[8,16,128]{2,1,0:T(8,128)} %stack.10), calls=%async_computation | async-start | bytes 131072 | tf_op jit(solution)/shard_map/all_to_all | solution.py:106
  62.4 92.2 %reduce-scatter.2.cloned.1.call-start = ((), (), s32[]{:S(2)}) async-start(), calls=%async_computation.2 | async-start | bytes 73728 | tf_op jit(solution)/shard_map/reduce_scatter | solution.py:132
  77.1 362.5 %all-reduce.7.cloned.1.call-start = ((), (), s32[]{:S(2)}) async-start(), calls=%async_computation.3 | async-start | bytes 6815744 | tf_op jit(solution)/shard_map/psum | solution.py:146
  154.7 8.1 %copy-start.1 = (f32[2048,512]{1,0:T(8,128)S(1)}, f32[2048,512]{1,0:T(8,128)}, u32[]{:S(2)}) copy-start(f32[2048,512]{1,0:T(8,128)} %add_add_fusion) | copy-start | bytes 12582916
  162.8 2.7 copy-start.6
  165.6 3.7 copy-start.2
  166.9 2.3 copy-start.7
  172.4 3.1 copy-start.3
  172.5 3.1 copy-start.8
  439.6 3.9 copy-start.9
Sparse Core Ops, SparseCore 0:
  77.2 77.4 reduce-scatter.1
  172.6 266.9 all-reduce.6
